TPU v7x, 32 devices: a whole 2x2x4 slice. The times are simulated.
32 devices in a mesh: va: 8 (over y, x, core), vb: 4 (over z).
Axes of the slice: x: 2, y: 2, z: 4, core: 2. Of those that a mesh axis runs over, the one named last changes fastest.
Arguments:
- clique_a: float32 [16, 8, 2, 16, 32768], P('va', 'vb'), may hold values from 0.2 to 5
- message_in: float32 [16, 2, 32768], P('va'), may hold values from 0.2 to 5
- clique_b: float32 [32, 8, 16, 16, 8, 256], P(None, None, None, 'va', 'vb'), may hold values from 0.2 to 5
- old_separator: float32 [8, 16, 16, 8, 256], P(None, None, 'va', 'vb'), may hold values from 0.25 to 4
Outputs:
- absorbed: float32 [16, 8, 2, 16, 32768], P('va', 'vb')
- updated_b: float32 [32, 8, 16, 16, 8, 256], P(None, None, None, 'va', 'vb')
- onward: float32 [32, 16, 16, 256], P('vb', None, 'va')
All inputs are finite; a program needn't handle non-finite values.
Results may differ from a plain program's by a relative error of at most 0.00002.
Values sent between devices are 32-bit elements; how exact they have to be, the bound alone decides.
No kernel may reach another device: no remote copies, remote signals or barrier semaphores. Data moves between devices by JAX's collectives and lax.ppermute only.
A program may use at most 192 MiB of HBM per device.

v0:
```python
import jax
import jax.numpy as jnp
from jax import lax
from jax.sharding import PartitionSpec as P

H = 16
K = 2
P_SIZE = 8
R1 = 16
R2 = 8
R3 = 256


def body(clique_a, message_in, clique_b, old_separator):
    p_local = clique_a.shape[1]
    q_total = clique_a.shape[3]
    r_total = clique_a.shape[4]
    absorbed = clique_a * message_in[:, None, :, None, :]
    column_width = r_total // R1
    summed = jnp.sum(absorbed, axis=(0, 2)) * (1.0 / (H * K))
    summed = summed.reshape(
        p_local, q_total, lax.axis_size("va") * (R1 // lax.axis_size("va")), column_width
    )
    shares = lax.psum_scatter(
        jnp.transpose(summed, (2, 0, 1, 3)), "va", scatter_dimension=0, tiled=True
    )
    shares = shares.reshape(shares.shape[0], p_local, q_total, R2, R3)
    moved = lax.all_to_all(shares, "vb", split_axis=3, concat_axis=1, tiled=True)
    separator = jnp.transpose(moved, (1, 2, 0, 3, 4))
    scaling = separator / old_separator
    updated_b = clique_b * scaling[None]
    partial_value = jnp.sum(updated_b, axis=(1, 4)) * (1.0 / (P_SIZE * R2))
    onward = lax.psum_scatter(partial_value, "vb", scatter_dimension=0, tiled=True)
    return (absorbed, updated_b, onward)


def solution(mesh):
    return jax.shard_map(
        body,
        mesh=mesh,
        in_specs=(
            P("va", "vb", None, None, None),
            P("va", None, None),
            P(None, None, None, "va", "vb", None),
            P(None, None, "va", "vb", None),
        ),
        out_specs=(
            P("va", "vb", None, None, None),
            P(None, None, None, "va", "vb", None),
            P("vb", None, "va", None),
        ),
        check_vma=False,
    )
```

profile of v0, /device:TPU:0, one launch (start us, length us, event | category | flops | bytes accessed | tf_op | source)
XLA Modules:
  0.0 156.1 jit_solution(7697594367874494386)
XLA Ops:
  7.2 0.0 reduce-scatter.3.cloned.1.call-start
  7.2 12.5 %fusion.1 = (f32[2,16,32768]{2,1,0:T(8,128)S(1)}, f32[2,2,2,16,32768]{4,3,2,1,0:T(8,128)}) fusion(f32[2,2,2,16,32768]{4,3,2,1,0:T(8,128)} %param.4, f32[2,2,32768]{2,1,0:T(2,128)} %param.5), kind=kLoop, calls=%fused_computation.8 | loop fusion | flops 7340032 | bytes 38273024 | tf_op jit(solution)/shard_map/reduce_sum | solution.py:20
  19.7 0.3 broadcast_multiply_fusion.2
  19.9 0.0 copy-start
  19.9 2.4 %copy.41 = f32[4,8,16,2048]{3,2,1,0:T(8,128)S(1)} copy(f32[4,8,16,2048]{3,1,2,0:T(8,128)S(1)} %bitcast.18) | data formatting | bytes 8388608
  22.4 0.5 bitcast_bitcast_fusion
  22.9 4.4 %copy.31 = f32[16,2,16,2048]{3,2,1,0:T(8,128)} copy(f32[16,2,16,2048]{3,0,2,1:T(8,128)S(1)} %bitcast_bitcast_fusion) | data formatting | bytes 8388608 | tf_op jit(solution)/shard_map/transpose | solution.py:25
  27.3 0.0 reduce-scatter.3.cloned.1.call-update
  27.4 0.0 reduce-scatter.5.cloned.1.call-start
  27.4 54.1 %reduce-scatter.3.cloned.1.call-done = f32[2,2,16,2048]{3,2,1,0:T(8,128)} async-done(((f32[16,2,16,2048]{3,2,1,0:T(8,128)}), f32[2,2,16,2048]{3,2,1,0:T(8,128)}) %reduce-scatter.3.cloned.1.call-update) | async-done | bytes 524304 | tf_op jit(solution)/shard_map/reduce_scatter | solution.py:24
  81.5 1.1 copy.45
  82.6 18.9 %all_to_all.18 = f32[2,2,16,8,256]{4,2,1,0,3:T(8,128)S(1)} all-to-all(f32[2,2,16,8,256]{4,2,1,0,3:T(8,128)S(1)} %bitcast.21), channel_id=1, replica_groups=mesh['va'=8,'vb'=4] {'vb'}, dimensions={3} | all-to-all | bytes 1048576 | tf_op jit(solution)/shard_map/all_to_all | solution.py:28
  101.6 0.0 copy-done
  101.6 0.1 copy_divide_fusion
  101.7 0.4 copy.36
  102.1 18.7 %fusion = (f32[32,16,2,256]{3,2,1,0:T(2,128)S(1)}, f32[32,8,16,2,2,256]{5,4,3,2,1,0:T(2,128)}) fusion(f32[32,8,16,2,2,256]{5,4,3,2,1,0:T(2,128)} %param.6, f32[8,16,2,2,256]{4,3,2,1,0:T(2,128)S(1)} %copy.36), kind=kLoop, calls=%fused_computation.7 | loop fusion | flops 8126464 | bytes 35127296 | tf_op jit(solution)/shard_map/reduce_sum | solution.py:32
  120.9 1.1 copy_multiply_fusion
  122.0 0.0 reduce-scatter.5.cloned.1.call-update
  122.0 25.4 %reduce-scatter.5.cloned.1.call-done = f32[8,16,2,256]{3,1,2,0:T(8,128)} async-done(((f32[32,16,2,256]{3,1,2,0:T(8,128)}), f32[8,16,2,256]{3,1,2,0:T(8,128)}) %reduce-scatter.5.cloned.1.call-update) | async-done | bytes 262160 | tf_op jit(solution)/shard_map/reduce_scatter | solution.py:33
  147.5 1.9 %copy.38 = f32[8,16,2,256]{3,2,1,0:T(2,128)} copy(f32[8,16,2,256]{3,1,2,0:T(8,128)} %reduce-scatter.5.cloned.1.call-done) | data formatting | bytes 524288
  (1 shorter events, 0.0 us)
Async XLA Ops:
  7.2 74.4 %reduce-scatter.3.cloned.1.call-start = ((), (), s32[]{:S(2)}) async-start(), calls=%async_computation.3 | async-start | bytes 4718592 | tf_op jit(solution)/shard_map/reduce_scatter | solution.py:24
  19.9 81.6 %copy-start = (f32[8,16,2,2,256]{4,3,2,1,0:T(2,128)S(1)}, f32[8,16,2,2,256]{4,3,2,1,0:T(2,128)}, u32[]{:S(2)}) copy-start(f32[8,16,2,2,256]{4,3,2,1,0:T(2,128)} %param.7) | copy-start | bytes 1572868
  27.4 120.1 %reduce-scatter.5.cloned.1.call-start = ((), (), s32[]{:S(2)}) async-start(), calls=%async_computation.4 | async-start | bytes 1310720 | tf_op jit(solution)/shard_map/reduce_scatter | solution.py:33
Sparse Core Ops, SparseCore 0:
  27.5 53.9 reduce-scatter.2
  122.2 25.2 reduce-scatter.4
where the time goes:
time: 156 us
  waiting for transfers between devices  79.6 us (51%)
  other arithmetic  32.7 us (21%)
  blocking collectives  18.9 us (12%)
  between operations  14.1 us (9%)
  local copies, waits for them, and re-layouts  10.8 us (7%)
    reduce_scatter x1, waiting for transfers between devices, body(): lax.psum_scatter(jnp.transpose(summed, (2, 0, 1, 3)), 'va', scatter_dimen...  54.1 us
    reduce_scatter x1, waiting for transfers between devices, body(): lax.psum_scatter(partial_value, 'vb', scatter_dimension=0, tiled=True)  25.4 us
    all_to_all x1, blocking collectives, body(): lax.all_to_all(shares, 'vb', split_axis=3, concat_axis=1, tiled=True)  18.9 us
    reduce_sum x1, other arithmetic, body(): partial_value = jnp.sum(updated_b, axis=(1, 4)) * (1.0 / (P_SIZE * R2))  18.7 us
    reduce_sum x1, other arithmetic, body(): summed = jnp.sum(absorbed, axis=(0, 2)) * (1.0 / (H * K))  12.5 us
    transpose x2, local copies, waits for them, and re-layouts, body(): jnp.transpose(summed, (2, 0, 1, 3))  4.93 us
    unnamed x4, local copies, waits for them, and re-layouts  4.29 us
  transfers between devices with their start and end apart: 2, of which 2 were waited for; matrix products, arithmetic and copies ran while one was open for 0% of the time, Pallas kernels for 0%

commit v1 on v0

--- a/solution.py
+++ b/solution.py
@@ -2,6 +2,7 @@
 import jax.numpy as jnp
 from jax import lax
 from jax.sharding import PartitionSpec as P
+from jax.lax import axis_index, axis_size, ppermute
 
 H = 16
 K = 2
@@ -25,7 +26,21 @@
         jnp.transpose(summed, (2, 0, 1, 3)), "va", scatter_dimension=0, tiled=True
     )
     shares = shares.reshape(shares.shape[0], p_local, q_total, R2, R3)
-    moved = lax.all_to_all(shares, "vb", split_axis=3, concat_axis=1, tiled=True)
+    far_arr, arr_now = (axis_size("vb"), axis_index("vb"))
+    even = list(shares.shape)
+    finding = shares.shape[3] // far_arr
+    even[3] = finding
+    piece_now = even[1]
+    even[1] = piece_now * far_arr
+    moved = jnp.zeros(even, shares.dtype)
+    for ii in range(far_arr):
+        q_next = lax.dynamic_slice_in_dim(shares, (arr_now ^ ii) * finding, finding, axis=3)
+        if ii:
+            inbox = []
+            for k0 in range(far_arr):
+                inbox.append((k0, k0 ^ ii))
+            q_next = ppermute(q_next, "vb", inbox)
+        moved = lax.dynamic_update_slice_in_dim(moved, q_next, (arr_now ^ ii) * piece_now, axis=1)
     separator = jnp.transpose(moved, (1, 2, 0, 3, 4))
     scaling = separator / old_separator
     updated_b = clique_b * scaling[None]

time: 156 us -> 154 us (0.987)
  blocking collectives: 18.9 us -> 0 us
  waiting for transfers between devices: 79.6 us -> 90.7 us
  starting transfers between devices: 0.08 us -> 4.53 us
    all_to_all x1 -> x0, blocking collectives: 18.9 us -> none  [body(): lax.all_to_all(shares, 'vb', split_axis=3, concat_axis=1, tiled=True)]
    ppermute x0 -> x3, waiting for transfers between devices: none -> 9.82 us  [body(): q_next = ppermute(q_next, 'vb', inbox)]
    ppermute x0 -> x3, starting transfers between devices: none -> 4.45 us  [body(): q_next = ppermute(q_next, 'vb', inbox)]
    unnamed x4 -> x8, local copies, waits for them, and re-layouts: 4.29 us -> 5.57 us
  transfers between devices with their start and end apart: 2 -> 5, of which waited for: 2 -> 4; matrix products, arithmetic and copies ran while one was open for 0% -> 0% of each run, Pallas kernels for 0% -> 0%
where the time goes in v1:
time: 154 us; the launch traced here: 153 us
  waiting for transfers between devices  90.7 us (59%)
  other arithmetic  32.9 us (21%)
  between operations  14.2 us (9%)
  local copies, waits for them, and re-layouts  11 us (7%)
  starting transfers between devices  4.53 us (3%)
    reduce_scatter x1, waiting for transfers between devices, body(): lax.psum_scatter(jnp.transpose(summed, (2, 0, 1, 3)), 'va', scatter_dimen...  54.1 us
    reduce_scatter x1, waiting for transfers between devices, body(): lax.psum_scatter(partial_value, 'vb', scatter_dimension=0, tiled=True)  26.8 us
    reduce_sum x1, other arithmetic, body(): partial_value = jnp.sum(updated_b, axis=(1, 4)) * (1.0 / (P_SIZE * R2))  18.7 us
    reduce_sum x1, other arithmetic, body(): summed = jnp.sum(absorbed, axis=(0, 2)) * (1.0 / (H * K))  12.5 us
    ppermute x3, waiting for transfers between devices, body(): q_next = ppermute(q_next, 'vb', inbox)  9.82 us
    unnamed x8, local copies, waits for them, and re-layouts  5.57 us
    transpose x2, local copies, waits for them, and re-layouts, body(): jnp.transpose(summed, (2, 0, 1, 3))  4.93 us
    ppermute x3, starting transfers between devices, body(): q_next = ppermute(q_next, 'vb', inbox)  4.45 us
  transfers between devices with their start and end apart: 5, of which 4 were waited for; matrix products, arithmetic and copies ran while one was open for 0% of the time, Pallas kernels for 0%

profile of v1, /device:TPU:0, one launch (start us, length us, event | category | flops | bytes accessed | tf_op | source)
XLA Modules:
  0.0 153.3 jit_solution(8405900124823397670)
XLA Ops:
  7.2 0.0 reduce-scatter.3.cloned.1.call-start
  7.2 12.5 %fusion.1 = (f32[2,16,32768]{2,1,0:T(8,128)S(1)}, f32[2,2,2,16,32768]{4,3,2,1,0:T(8,128)}) fusion(f32[2,2,2,16,32768]{4,3,2,1,0:T(8,128)} %param.4, f32[2,2,32768]{2,1,0:T(2,128)} %param.5), kind=kLoop, calls=%fused_computation.15 | loop fusion | flops 7340032 | bytes 38273024 | tf_op jit(solution)/shard_map/reduce_sum | solution.py:21
  19.7 0.3 broadcast_multiply_fusion.2
  19.9 0.0 copy-start
  19.9 2.4 %copy.36 = f32[4,8,16,2048]{3,2,1,0:T(8,128)S(1)} copy(f32[4,8,16,2048]{3,1,2,0:T(8,128)S(1)} %bitcast.15) | data formatting | bytes 8388608
  22.4 0.5 bitcast_bitcast_fusion
  22.9 4.4 %copy.25 = f32[16,2,16,2048]{3,2,1,0:T(8,128)} copy(f32[16,2,16,2048]{3,0,2,1:T(8,128)S(1)} %bitcast_bitcast_fusion) | data formatting | bytes 8388608 | tf_op jit(solution)/shard_map/transpose | solution.py:26
  27.3 0.0 reduce-scatter.3.cloned.1.call-update
  27.4 0.0 reduce-scatter.5.cloned.1.call-start
  27.4 54.1 %reduce-scatter.3.cloned.1.call-done = f32[2,2,16,2048]{3,2,1,0:T(8,128)} async-done(((f32[16,2,16,2048]{3,2,1,0:T(8,128)}), f32[2,2,16,2048]{3,2,1,0:T(8,128)}) %reduce-scatter.3.cloned.1.call-update) | async-done | bytes 524304 | tf_op jit(solution)/shard_map/reduce_scatter | solution.py:25
  81.5 1.2 copy.37
  82.7 0.2 constant_dynamic-slice_fusion
  83.1 1.5 %collective-permute-start = (f32[2,2,16,2,256]{4,3,0,2,1:T(2,128)S(1)}, f32[2,2,16,2,256]{4,3,0,2,1:T(2,128)S(1)}, u32[]{:S(2)}, u32[]{:S(2)}) collective-permute-start(f32[2,2,16,2,256]{4,3,0,2,1:T(2,128)S(1)} %copy.33), channel_id=1, source_target_pairs={{0,1},{1,0},{2,3},{3,2},{4,5},{5,4},{6,7},{7,6},{8,9},{9,8},{10,11... | collective-permute-start | bytes 393224 | tf_op jit(solution)/shard_map/ppermute | solution.py:42
  84.6 2.4 %collective-permute-start.1 = (f32[2,2,16,2,256]{4,3,0,2,1:T(2,128)S(1)}, f32[2,2,16,2,256]{4,3,0,2,1:T(2,128)S(1)}, u32[]{:S(2)}, u32[]{:S(2)}) collective-permute-start(f32[2,2,16,2,256]{4,3,0,2,1:T(2,128)S(1)} %copy.34), channel_id=1, source_target_pairs={{0,2},{1,3},{2,0},{3,1},{4,6},{5,7},{6,4},{7,5},{8,10},{9,11},{10,... | collective-permute-start | bytes 393224 | tf_op jit(solution)/shard_map/ppermute | solution.py:42
  87.0 0.5 collective-permute-start.2
  87.5 0.1 broadcast_in_dim.2
  87.7 2.3 %collective-permute-done = f32[2,2,16,2,256]{4,3,0,2,1:T(2,128)S(1)} collective-permute-done((f32[2,2,16,2,256]{4,3,0,2,1:T(2,128)S(1)}, f32[2,2,16,2,256]{4,3,0,2,1:T(2,128)S(1)}, u32[]{:S(2)}, u32[]{:S(2)}) %collective-permute-start) | collective-permute-done | bytes 131104 | tf_op jit(solution)/shard_map/ppermute | solution.py:42
  90.0 7.6 %collective-permute-done.1 = f32[2,2,16,2,256]{4,3,0,2,1:T(2,128)S(1)} collective-permute-done((f32[2,2,16,2,256]{4,3,0,2,1:T(2,128)S(1)}, f32[2,2,16,2,256]{4,3,0,2,1:T(2,128)S(1)}, u32[]{:S(2)}, u32[]{:S(2)}) %collective-permute-start.1) | collective-permute-done | bytes 131104 | tf_op jit(solution)/shard_map/ppermute | solution.py:42
  97.6 0.3 bitcast_divide_fusion
  97.9 18.7 %fusion = (f32[32,16,2,256]{3,2,1,0:T(2,128)S(1)}, f32[32,8,16,2,2,256]{5,4,3,2,1,0:T(2,128)}) fusion(f32[32,8,16,2,2,256]{5,4,3,2,1,0:T(2,128)} %param.6, f32[8,16,2,2,256]{4,3,2,1,0:T(2,128)S(1)} %bitcast_divide_fusion), kind=kLoop, calls=%fused_computation.14 | loop fusion | flops 8126464 | bytes 35127296 | tf_op jit(solution)/shard_map/reduce_sum | solution.py:47
  116.7 1.1 copy_multiply_fusion
  117.8 0.0 reduce-scatter.5.cloned.1.call-update
  117.8 26.8 %reduce-scatter.5.cloned.1.call-done = f32[8,16,2,256]{3,1,2,0:T(8,128)} async-done(((f32[32,16,2,256]{3,1,2,0:T(8,128)}), f32[8,16,2,256]{3,1,2,0:T(8,128)}) %reduce-scatter.5.cloned.1.call-update) | async-done | bytes 262160 | tf_op jit(solution)/shard_map/reduce_scatter | solution.py:48
  144.6 1.9 %copy.31 = f32[8,16,2,256]{3,2,1,0:T(2,128)} copy(f32[8,16,2,256]{3,1,2,0:T(8,128)} %reduce-scatter.5.cloned.1.call-done) | data formatting | bytes 524288
  (9 shorter events, 0.2 us)
Async XLA Ops:
  7.2 74.4 %reduce-scatter.3.cloned.1.call-start = ((), (), s32[]{:S(2)}) async-start(), calls=%async_computation.2 | async-start | bytes 4718592 | tf_op jit(solution)/shard_map/reduce_scatter | solution.py:25
  19.9 77.7 %copy-start = (f32[8,16,2,2,256]{4,3,2,1,0:T(2,128)S(1)}, f32[8,16,2,2,256]{4,3,2,1,0:T(2,128)}, u32[]{:S(2)}) copy-start(f32[8,16,2,2,256]{4,3,2,1,0:T(2,128)} %param.7) | copy-start | bytes 1572868
  27.4 117.3 %reduce-scatter.5.cloned.1.call-start = ((), (), s32[]{:S(2)}) async-start(), calls=%async_computation.3 | async-start | bytes 1310720 | tf_op jit(solution)/shard_map/reduce_scatter | solution.py:48
  83.1 6.9 %collective-permute-start = (f32[2,2,16,2,256]{4,3,0,2,1:T(2,128)S(1)}, f32[2,2,16,2,256]{4,3,0,2,1:T(2,128)S(1)}, u32[]{:S(2)}, u32[]{:S(2)}) collective-permute-start(f32[2,2,16,2,256]{4,3,0,2,1:T(2,128)S(1)} %copy.33), channel_id=1, source_target_pairs={{0,1},{1,0},{2,3},{3,2},{4,5},{5,4},{6,7},{7,6},{8,9},{9,8},{10,11... | collective-permute-start | bytes 393224 | tf_op jit(solution)/shard_map/ppermute | solution.py:42
  84.6 12.9 %collective-permute-start.1 = (f32[2,2,16,2,256]{4,3,0,2,1:T(2,128)S(1)}, f32[2,2,16,2,256]{4,3,0,2,1:T(2,128)S(1)}, u32[]{:S(2)}, u32[]{:S(2)}) collective-permute-start(f32[2,2,16,2,256]{4,3,0,2,1:T(2,128)S(1)} %copy.34), channel_id=1, source_target_pairs={{0,2},{1,3},{2,0},{3,1},{4,6},{5,7},{6,4},{7,5},{8,10},{9,11},{10,... | collective-permute-start | bytes 393224 | tf_op jit(solution)/shard_map/ppermute | solution.py:42
  87.0 10.5 %collective-permute-start.2 = (f32[2,2,16,2,256]{4,3,0,2,1:T(2,128)S(1)}, f32[2,2,16,2,256]{4,3,0,2,1:T(2,128)S(1)}, u32[]{:S(2)}, u32[]{:S(2)}) collective-permute-start(f32[2,2,16,2,256]{4,3,0,2,1:T(2,128)S(1)} %copy.35), channel_id=1, source_target_pairs={{0,3},{1,2},{2,1},{3,0},{4,7},{5,6},{6,5},{7,4},{8,11},{9,10},{10,... | collective-permute-start | bytes 393224 | tf_op jit(solution)/shard_map/ppermute | solution.py:42
Sparse Core Ops, SparseCore 0:
  27.5 53.9 reduce-scatter.2
  117.9 26.6 reduce-scatter.4
